TPU v7x, 32 devices: a whole 2x2x4 slice. The times are simulated.
32 devices in a mesh: row: 8 (over z, y), col: 4 (over x, core).
Axes of the slice: x: 2, y: 2, z: 4, core: 2. Of those that a mesh axis runs over, the one named last changes fastest.
Arguments:
- amplitudes: float32 [64, 2, 640], P('row', None, 'col'), may hold values from -6 to 6
- integrals: float32 [2, 640, 640, 640], P(None, 'col', 'row'), may hold values from -0.5 to 0.5
- virt_irrep: int32 [640], replicated, may hold values from 0 to 7
- pair_irrep: int32 [64], replicated, may hold values from 0 to 7
- tile_mask: int32 [8, 8], replicated, may hold values 0 or 1
Outputs:
- residual: float32 [64, 640, 640], P('col', 'row')
All inputs are finite; a program needn't handle non-finite values.
Results may differ from a plain program's by a relative error of at most 0.000071.
Values sent between devices are 32-bit elements; how exact they have to be, the bound alone decides.
A program may use at most 192 MiB of HBM per device.

v0:
```python
import jax
import jax.numpy as jnp
from jax import lax
from jax.sharding import PartitionSpec as P


def reduce_pairs(partial_sums):
    return lax.psum_scatter(partial_sums, "col", scatter_dimension=0, tiled=True)


def mirror_after(owned):
    swapped = lax.all_to_all(owned, "row", split_axis=2, concat_axis=1, tiled=True)
    return owned - jnp.transpose(swapped, (0, 2, 1))


def mask_slab(amps, c_labels, d_labels, pair_irrep, tile_mask):
    labels_range = jnp.arange(tile_mask.shape[0], dtype=jnp.int32)
    c_onehot = (c_labels[:, None] == labels_range[None, :]).astype(jnp.float32)
    d_onehot = (d_labels[:, None] == labels_range[None, :]).astype(jnp.float32)
    tile_float = tile_mask.astype(jnp.float32)
    screen = jnp.dot(
        jnp.dot(
            c_onehot,
            tile_float,
            precision=lax.Precision.HIGHEST,
            preferred_element_type=jnp.float32,
        ),
        d_onehot.T,
        precision=lax.Precision.HIGHEST,
        preferred_element_type=jnp.float32,
    )
    allowed = (
        jnp.bitwise_xor(c_labels[:, None], d_labels[None, :])[None, :, :]
        == pair_irrep[:, None, None]
    )
    return amps * screen[None, :, :] * allowed.astype(jnp.float32)


def local(amplitudes, integrals, virt_irrep, pair_irrep, tile_mask):
    slab_width = amplitudes.shape[1]
    d_width = integrals.shape[1]
    a_width = integrals.shape[2]
    full_width = integrals.shape[3]
    row_index = lax.axis_index("row")
    col_index = lax.axis_index("col")
    gathered = lax.all_gather(amplitudes, "row", axis=0, tiled=True)
    pair_count = gathered.shape[0]
    c_labels = virt_irrep[:slab_width]
    d_labels = lax.dynamic_slice_in_dim(virt_irrep, col_index * d_width, d_width)
    masked = mask_slab(gathered, c_labels, d_labels, pair_irrep, tile_mask)
    partial_sums = jnp.dot(
        masked.reshape(pair_count, slab_width * d_width),
        integrals.reshape(slab_width * d_width, a_width * full_width),
        precision=lax.Precision.HIGHEST,
        preferred_element_type=jnp.float32,
    ).reshape(pair_count, a_width, full_width)
    mirrored = mirror_after(reduce_pairs(partial_sums))
    own_pairs = mirrored.shape[0]
    a_labels = lax.dynamic_slice_in_dim(virt_irrep, row_index * a_width, a_width)
    pair_labels = lax.dynamic_slice_in_dim(pair_irrep, col_index * own_pairs, own_pairs)
    kept_mask = (
        jnp.bitwise_xor(a_labels[:, None], virt_irrep[None, :])[None, :, :]
        == pair_labels[:, None, None]
    )
    return mirrored * kept_mask.astype(jnp.float32)


def solution(mesh):
    in_specs = (P("row", None, "col"), P(None, "col", "row", None), P(), P(), P())
    out_specs = P("col", "row", None)
    return jax.shard_map(local, mesh=mesh, in_specs=in_specs, out_specs=out_specs, check_vma=False)
```

profile of v0, /device:TPU:0, one launch (start us, length us, event | category | flops | bytes accessed | tf_op | source)
XLA Modules:
  0.0 375.9 jit_solution(2555133089651261318)
XLA Ops:
  6.5 0.0 reduce-scatter.2.cloned.1.call-start
  6.5 0.7 slice.3
  7.2 0.8 dynamic_slice.11
  8.0 0.9 fusion.6
  8.9 0.1 broadcast_xor_fusion.1
  8.9 0.2 fusion.4
  9.1 32.6 %all_gather.3 = f32[64,2,160]{2,1,0:T(2,128)S(1)} all-gather(f32[8,2,160]{2,1,0:T(2,128)} %param.5), channel_id=1, replica_groups=mesh['row'=8,'col'=4] {'row'}, dimensions={0}, use_global_device_ids=true | all-gather | bytes 92160 | tf_op jit(solution)/shard_map/all_gather | solution.py:46
  41.7 0.8 compare_select_fusion
  42.5 0.1 reshape.68
  42.7 79.4 %fusion = f32[64,80,640]{2,0,1:T(8,128)} fusion(f32[64,320,1]{1,0,2:T(8,128)S(1)} %reshape.68, f32[40,8,80,640]{3,2,1,0:T(8,128)} %bitcast.26), kind=kOutput, calls=%fused_computation | convolution fusion | flops 12582912000 | bytes 78725120 | tf_op jit(solution)/shard_map/dot_general | solution.py:51
  122.1 0.0 reduce-scatter.2.cloned.1.call-update
  122.2 101.4 %reduce-scatter.2.cloned.1.call-done = f32[16,80,640]{2,0,1:T(8,128)} async-done(((f32[64,80,640]{2,0,1:T(8,128)}), f32[16,80,640]{2,0,1:T(8,128)}) %reduce-scatter.2.cloned.1.call-update) | async-done | bytes 3276816 | tf_op jit(solution)/shard_map/reduce_scatter | solution.py:8
  223.6 5.6 %copy.16 = f32[16,80,640]{1,0,2:T(8,128)} copy(f32[16,80,640]{2,0,1:T(8,128)} %reduce-scatter.2.cloned.1.call-done) | data formatting | bytes 6553600 | tf_op jit(solution)/shard_map/reduce_scatter | solution.py:8
  229.2 0.0 copy-start.2
  229.2 0.0 copy-start.1
  229.2 5.6 %all-to-all-start = ((f32[16,80,640]{1,0,2:T(8,128)}), f32[16,80,640]{1,0,2:T(8,128)}, u32[]{:S(2)}, u32[]{:S(2)}) async-start(f32[16,80,640]{1,0,2:T(8,128)} %copy.16), calls=%async_computation.1 | async-start | bytes 10485760 | tf_op jit(solution)/shard_map/all_to_all | solution.py:12
  234.8 0.0 copy-done.2
  234.9 0.1 dynamic_slice.10
  234.9 0.0 copy-done.1
  234.9 0.1 dynamic_slice.9
  235.0 0.1 broadcast_xor_fusion
  235.1 115.3 %all-to-all-done = f32[16,80,640]{1,0,2:T(8,128)} async-done(((f32[16,80,640]{1,0,2:T(8,128)}), f32[16,80,640]{1,0,2:T(8,128)}, u32[]{:S(2)}, u32[]{:S(2)}) %all-to-all-start) | async-done | bytes 3276832 | tf_op jit(solution)/shard_map/all_to_all | solution.py:12
  350.4 7.9 %copy.29 = f32[16,80,8,80]{1,2,0,3:T(8,128)} copy(f32[16,80,8,80]{1,0,3,2:T(8,128)} %bitcast.1) | data formatting | bytes 6553600 | tf_op jit(solution)/shard_map/all_to_all | solution.py:12
  358.3 0.0 copy-start
  358.3 5.5 %all_to_all.16 = f32[16,640,80]{1,0,2:T(8,128)} reshape(f32[16,8,80,80]{2,1,0,3:T(8,128)} %bitcast.27) | data formatting | bytes 6553600 | tf_op jit(solution)/shard_map/all_to_all | solution.py:12
  363.8 0.0 copy-done
  363.8 2.5 fusion.3
  366.4 2.7 copy.18
Async XLA Ops:
  6.5 217.0 %reduce-scatter.2.cloned.1.call-start = ((), (), s32[]{:S(2)}) async-start(), calls=%async_computation.2 | async-start | bytes 16384000 | tf_op jit(solution)/shard_map/reduce_scatter | solution.py:8
  229.2 5.6 %copy-start.2 = (s32[64]{0:T(128)S(1)}, s32[64]{0:T(128)}, u32[]{:S(2)}) copy-start(s32[64]{0:T(128)} %param.8) | copy-start | bytes 772
  229.2 5.7 %copy-start.1 = (s32[640]{0:T(1024)S(1)}, s32[640]{0:T(1024)}, u32[]{:S(2)}) copy-start(s32[640]{0:T(1024)} %param.7) | copy-start | bytes 7684
  229.2 121.2 %all-to-all-start = ((f32[16,80,640]{1,0,2:T(8,128)}), f32[16,80,640]{1,0,2:T(8,128)}, u32[]{:S(2)}, u32[]{:S(2)}) async-start(f32[16,80,640]{1,0,2:T(8,128)} %copy.16), calls=%async_computation.1 | async-start | bytes 10485760 | tf_op jit(solution)/shard_map/all_to_all | solution.py:12
  358.3 5.5 %copy-start = (f32[16,80,640]{2,0,1:T(8,128)S(1)}, f32[16,80,640]{2,0,1:T(8,128)}, u32[]{:S(2)}) copy-start(f32[16,80,640]{2,0,1:T(8,128)} %reduce-scatter.2.cloned.1.call-done) | copy-start | bytes 9830404
Sparse Core Ops, SparseCore 0:
  122.3 101.2 reduce-scatter.1
where the time goes:
time: 376 us
  waiting for transfers between devices  217 us (58%)
  matrix products  80.5 us (21%)
  blocking collectives  32.6 us (9%)
  local copies, waits for them, and re-layouts  23.5 us (6%)
  between operations  13.4 us (4%)
  starting transfers between devices  5.64 us (2%)
    all_to_all x1, waiting for transfers between devices, mirror_after(): lax.all_to_all(owned, 'row', split_axis=2, concat_axis=1, tiled=True)  115 us
    reduce_scatter x1, waiting for transfers between devices, reduce_pairs(): lax.psum_scatter(partial_sums, 'col', scatter_dimension=0, tiled=True)  101 us
    dot_general x1, matrix products, local(): jnp.dot(masked.reshape(pair_count, slab_width * d_width), integrals.resha...  79.4 us
    all_gather x1, blocking collectives, local(): gathered = lax.all_gather(amplitudes, 'row', axis=0, tiled=True)  32.6 us
    all_to_all x2, local copies, waits for them, and re-layouts, mirror_after(): lax.all_to_all(owned, 'row', split_axis=2, concat_axis=1, tiled=True)  13.4 us
  transfers between devices with their start and end apart: 2, of which 2 were waited for; matrix products, arithmetic and copies ran while one was open for 0% of the time, Pallas kernels for 0%

commit v1 on v0

--- a/solution.py
+++ b/solution.py
@@ -2,6 +2,29 @@
 import jax.numpy as jnp
 from jax import lax
 from jax.sharding import PartitionSpec as P
+
+
+def in_order(parts, dim):
+    shape = list(parts.shape[1:])
+    shape[dim] *= parts.shape[0]
+    return jnp.moveaxis(parts, 0, dim).reshape(shape)
+
+
+def doubled(x, axis):
+    peers, index = (lax.axis_size(axis), lax.axis_index(axis))
+    blocks, distance = (x[None], 1)
+    while distance < peers:
+        received = lax.ppermute(blocks, axis, [(i, i ^ distance) for i in range(peers)])
+        low = index & distance == 0
+        blocks = jnp.concatenate(
+            [jnp.where(low, blocks, received), jnp.where(low, received, blocks)]
+        )
+        distance *= 2
+    return blocks
+
+
+def gather_by_bits(x, axis, dim):
+    return in_order(doubled(x, axis), dim)
 
 
 def reduce_pairs(partial_sums):
@@ -43,7 +66,7 @@
     full_width = integrals.shape[3]
     row_index = lax.axis_index("row")
     col_index = lax.axis_index("col")
-    gathered = lax.all_gather(amplitudes, "row", axis=0, tiled=True)
+    gathered = gather_by_bits(amplitudes, "row", 0)
     pair_count = gathered.shape[0]
     c_labels = virt_irrep[:slab_width]
     d_labels = lax.dynamic_slice_in_dim(virt_irrep, col_index * d_width, d_width)

time: 376 us -> 357 us (0.949)
  blocking collectives: 32.6 us -> 0 us
  starting transfers between devices: 5.64 us -> 13.1 us
  waiting for transfers between devices: 217 us -> 222 us
    all_gather x1 -> x0, blocking collectives: 32.6 us -> none  [local(): gathered = lax.all_gather(amplitudes, 'row', axis=0, tiled=True)]
    ppermute x0 -> x3, starting transfers between devices: none -> 7.49 us  [doubled(): lax.ppermute(blocks, axis, [(i, i ^ distance) for i in range(peers)])]
  transfers between devices with their start and end apart: 2 -> 5, of which waited for: 2 -> 4; matrix products, arithmetic and copies ran while one was open for 0% -> 1% of each run, Pallas kernels for 0% -> 0%
where the time goes in v1:
time: 357 us
  waiting for transfers between devices  222 us (62%)
  matrix products  80.6 us (23%)
  local copies, waits for them, and re-layouts  24.2 us (7%)
  between operations  13.5 us (4%)
  starting transfers between devices  13.1 us (4%)
  other arithmetic  3.69 us (1%)
    all_to_all x1, waiting for transfers between devices, mirror_after(): lax.all_to_all(owned, 'row', split_axis=2, concat_axis=1, tiled=True)  115 us
    reduce_scatter x1, waiting for transfers between devices, reduce_pairs(): lax.psum_scatter(partial_sums, 'col', scatter_dimension=0, tiled=True)  103 us
    dot_general x1, matrix products, local(): jnp.dot(masked.reshape(pair_count, slab_width * d_width), integrals.resha...  79.6 us
    all_to_all x2, local copies, waits for them, and re-layouts, mirror_after(): lax.all_to_all(owned, 'row', split_axis=2, concat_axis=1, tiled=True)  13.4 us
    ppermute x3, starting transfers between devices, doubled(): lax.ppermute(blocks, axis, [(i, i ^ distance) for i in range(peers)])  7.49 us
  transfers between devices with their start and end apart: 5, of which 4 were waited for; matrix products, arithmetic and copies ran while one was open for 1% of the time, Pallas kernels for 0%

profile of v1, /device:TPU:0, one launch (start us, length us, event | category | flops | bytes accessed | tf_op | source)
XLA Modules:
  0.0 356.7 jit_solution(8757597381620441023)
XLA Ops:
  6.5 0.0 reduce-scatter.2.cloned.1.call-start
  6.5 3.0 collective-permute-start
  9.5 0.7 slice.3
  10.2 0.9 fusion.6
  11.1 0.8 dynamic_slice.11
  11.9 0.0 collective-permute-done
  11.9 0.7 broadcast_select_fusion.5
  12.6 1.7 collective-permute-start.1
  14.4 0.2 fusion.4
  14.6 2.0 collective-permute-done.1
  16.7 2.8 collective-permute-start.2
  19.4 0.1 broadcast_xor_fusion.1
  19.5 0.7 eq.75
  20.2 1.7 collective-permute-done.2
  21.9 0.1 broadcast_select_fusion.1
  22.0 0.1 compare_select_fusion
  22.1 0.1 reshape.150
  22.3 79.6 %fusion = f32[64,80,640]{2,0,1:T(8,128)} fusion(f32[64,320,1]{1,0,2:T(8,128)S(1)} %reshape.150, f32[40,8,80,640]{3,2,1,0:T(8,128)} %bitcast.29), kind=kOutput, calls=%fused_computation | convolution fusion | flops 12582912000 | bytes 78725120 | tf_op jit(solution)/shard_map/dot_general | solution.py:74
  101.8 0.0 reduce-scatter.2.cloned.1.call-update
  101.9 102.5 %reduce-scatter.2.cloned.1.call-done = f32[16,80,640]{2,0,1:T(8,128)} async-done(((f32[64,80,640]{2,0,1:T(8,128)}), f32[16,80,640]{2,0,1:T(8,128)}) %reduce-scatter.2.cloned.1.call-update) | async-done | bytes 3276816 | tf_op jit(solution)/shard_map/reduce_scatter | solution.py:31
  204.4 5.6 %copy.16 = f32[16,80,640]{1,0,2:T(8,128)} copy(f32[16,80,640]{2,0,1:T(8,128)} %reduce-scatter.2.cloned.1.call-done) | data formatting | bytes 6553600 | tf_op jit(solution)/shard_map/reduce_scatter | solution.py:31
  210.0 5.6 %all-to-all-start = ((f32[16,80,640]{1,0,2:T(8,128)}), f32[16,80,640]{1,0,2:T(8,128)}, u32[]{:S(2)}, u32[]{:S(2)}) async-start(f32[16,80,640]{1,0,2:T(8,128)} %copy.16), calls=%async_computation.1 | async-start | bytes 10485760 | tf_op jit(solution)/shard_map/all_to_all | solution.py:35
  215.6 0.0 copy-done.1
  215.6 0.1 dynamic_slice.9
  215.7 0.0 copy-done.2
  215.7 0.1 dynamic_slice.10
  215.8 0.1 broadcast_xor_fusion
  215.9 115.4 %all-to-all-done = f32[16,80,640]{1,0,2:T(8,128)} async-done(((f32[16,80,640]{1,0,2:T(8,128)}), f32[16,80,640]{1,0,2:T(8,128)}, u32[]{:S(2)}, u32[]{:S(2)}) %all-to-all-start) | async-done | bytes 3276832 | tf_op jit(solution)/shard_map/all_to_all | solution.py:35
  331.2 7.9 %copy.29 = f32[16,80,8,80]{1,2,0,3:T(8,128)} copy(f32[16,80,8,80]{1,0,3,2:T(8,128)} %bitcast.2) | data formatting | bytes 6553600 | tf_op jit(solution)/shard_map/all_to_all | solution.py:35
  339.1 5.5 %all_to_all.16 = f32[16,640,80]{1,0,2:T(8,128)} reshape(f32[16,8,80,80]{2,1,0,3:T(8,128)} %bitcast.30) | data formatting | bytes 6553600 | tf_op jit(solution)/shard_map/all_to_all | solution.py:35
  344.6 2.5 fusion.3
  347.2 2.7 copy.18
  (7 shorter events, 0.1 us)
Async XLA Ops:
  6.5 197.8 %reduce-scatter.2.cloned.1.call-start = ((), (), s32[]{:S(2)}) async-start(), calls=%async_computation.2 | async-start | bytes 16384000 | tf_op jit(solution)/shard_map/reduce_scatter | solution.py:31
  6.5 5.3 %collective-permute-start = (f32[1,8,2,160]{3,2,1,0:T(2,128)}, f32[1,8,2,160]{3,2,1,0:T(2,128)S(1)}, u32[]{:S(2)}, u32[]{:S(2)}) collective-permute-start(f32[1,8,2,160]{3,2,1,0:T(2,128)} %bitcast.31), channel_id=1, source_target_pairs={{0,4},{4,0},{8,12},{12,8},{16,20},{20,16},{24,28},{28,24},{1,5},{5... | collective-permute-start | bytes 30728 | tf_op jit(solution)/shard_map/ppermute | solution.py:17
  12.6 4.0 %collective-permute-start.1 = (f32[2,8,2,160]{3,2,1,0:T(2,128)S(1)}, f32[2,8,2,160]{3,2,1,0:T(2,128)S(1)}, u32[]{:S(2)}, u32[]{:S(2)}) collective-permute-start(f32[2,8,2,160]{3,2,1,0:T(2,128)S(1)} %pad_maximum_fusion.1), channel_id=1, source_target_pairs={{0,8},{4,12},{8,0},{12,4},{16,24},{20,28},{24,16},{28,20},{1,9},{5... | collective-permute-start | bytes 61448 | tf_op jit(solution)/shard_map/ppermute | solution.py:17
  16.7 5.2 %collective-permute-start.2 = (f32[4,8,2,160]{3,2,1,0:T(2,128)S(1)}, f32[4,8,2,160]{3,2,1,0:T(2,128)S(1)}, u32[]{:S(2)}, u32[]{:S(2)}) collective-permute-start(f32[4,8,2,160]{3,2,1,0:T(2,128)S(1)} %pad_maximum_fusion), channel_id=1, source_target_pairs={{0,16},{4,20},{8,24},{12,28},{16,0},{20,4},{24,8},{28,12},{1,17},{... | collective-permute-start | bytes 122888 | tf_op jit(solution)/shard_map/ppermute | solution.py:17
  210.0 5.6 %copy-start.1 = (s32[640]{0:T(1024)S(1)}, s32[640]{0:T(1024)}, u32[]{:S(2)}) copy-start(s32[640]{0:T(1024)} %param.7) | copy-start | bytes 7684
  210.0 5.7 %copy-start.2 = (s32[64]{0:T(128)S(1)}, s32[64]{0:T(128)}, u32[]{:S(2)}) copy-start(s32[64]{0:T(128)} %param.8) | copy-start | bytes 772
  210.0 121.2 %all-to-all-start = ((f32[16,80,640]{1,0,2:T(8,128)}), f32[16,80,640]{1,0,2:T(8,128)}, u32[]{:S(2)}, u32[]{:S(2)}) async-start(f32[16,80,640]{1,0,2:T(8,128)} %copy.16), calls=%async_computation.1 | async-start | bytes 10485760 | tf_op jit(solution)/shard_map/all_to_all | solution.py:35
  339.1 5.5 %copy-start = (f32[16,80,640]{2,0,1:T(8,128)S(1)}, f32[16,80,640]{2,0,1:T(8,128)}, u32[]{:S(2)}) copy-start(f32[16,80,640]{2,0,1:T(8,128)} %reduce-scatter.2.cloned.1.call-done) | copy-start | bytes 9830404
Sparse Core Ops, SparseCore 0:
  102.0 102.3 reduce-scatter.1
